TPU v7x, 256 devices: a whole 4x4x8 slice. The times are simulated.
256 devices in a mesh: seq: 8 (over y, core), users: 32 (over x, z).
Axes of the slice: x: 4, y: 4, z: 8, core: 2. Of those that a mesh axis runs over, the one named last changes fastest.
Arguments:
- hidden: float32 [32, 8192, 512], P('users', 'seq'), may hold values from -256 to 256
- target: bfloat16 [32, 8192, 512], P('users', 'seq'), may hold values from -0.25 to 0.25
- pool_table: bfloat16 [8192, 512], P('users'), may hold values from -1 to 1
- pool_items: int32 [8192], P('users'), may hold values from 1 to 16383
- labels: int32 [32, 8192], P('users', 'seq'), may hold values from 1 to 16383
- chosen: int32 [32, 64, 8], P('users', 'seq'), may hold values from 0 to 31, all different within a row
- offsets: int32 [32, 5], P('users'), may hold values from 0 to 8192, as said below
Outputs:
- loss: float32 [], replicated
- grad_hidden: float32 [32, 8192, 512], P('users', 'seq')
- grad_table: float32 [8192, 512], P('users')
Inputs may be any that keep to these rules, and one draw needn't show every extreme that they name: Each row offsets[u] starts at 0 and rises strictly; its last entry is the number of live positions of group u, and equals 8192 in some group; positions from it on are padding. `chosen`: each position block names 8 different negative blocks.
All inputs are finite; a program needn't handle non-finite values.
Results may differ from a plain program's by a relative error of at most 0.003.
Values may be sent and summed in bfloat16 or wider, within the bound.
A program may use at most 192 MiB of HBM per device.

v0:
```python
import jax
import jax.numpy as jnp
from jax import lax
from jax.sharding import PartitionSpec as P

NB = 256
PB = 128


def history_weights(bounds, positions):
    starts = bounds[:-1]
    finish = bounds[1:]
    lengths = (finish - starts).astype(jnp.float32)
    inside = (positions[..., None] >= starts) & (positions[..., None] < finish)
    return jnp.sum(jnp.where(inside, 1.0 / lengths, 0.0), axis=-1)


def block_terms(states, target, labels, weights, chosen, pool_rows, pool_ids, factor):
    narrow = states.astype(jnp.bfloat16)
    negatives = jnp.take(pool_rows, chosen, axis=0).reshape(-1, pool_rows.shape[2])
    neg_items = jnp.take(pool_ids, chosen, axis=0).reshape(-1)
    scores = jnp.dot(narrow, negatives.T, preferred_element_type=jnp.float32)
    target_wide = target.astype(jnp.float32)
    positive = jnp.sum(narrow.astype(jnp.float32) * target_wide, axis=1)
    masked = jnp.where(neg_items[None, :] == labels[:, None], -1e30, scores)
    peak = jnp.maximum(positive, jnp.max(masked, axis=1))
    neg_exp = jnp.exp(masked - peak[:, None])
    pos_exp = jnp.exp(positive - peak)
    totals = pos_exp + jnp.sum(neg_exp, axis=1)
    cross = peak + jnp.log(totals) - positive
    coeff = weights * factor
    neg_grad = (coeff[:, None] * neg_exp / totals[:, None]).astype(jnp.bfloat16)
    pos_grad = coeff * (pos_exp / totals - 1.0)
    state_grad = (
        jnp.dot(neg_grad, negatives, preferred_element_type=jnp.float32)
        + pos_grad[:, None] * target_wide
    )
    pool_grad = jnp.dot(neg_grad.T, narrow, preferred_element_type=jnp.float32)
    pool_grad = pool_grad.reshape(chosen.shape[0], pool_rows.shape[1], pool_rows.shape[2])
    return (jnp.sum(weights * cross), state_grad, pool_grad)


def run_blocks(
    states,
    targets,
    label_rows,
    weights,
    picked,
    visit_order,
    live_count,
    pool_rows,
    pool_ids,
    factor,
):
    batched = jax.vmap(block_terms, in_axes=(0, 0, 0, 0, 0, None, None, None))
    rounds = (live_count + 3) // 4

    def advance(turn_index, carried):
        loss_acc, grad_acc, state_acc = carried
        slot_picks = lax.dynamic_slice_in_dim(visit_order, turn_index * 4, 4)
        picked_now = jnp.take(picked, slot_picks, axis=0)
        part_loss, state_grad, pool_grad = batched(
            jnp.take(states, slot_picks, axis=0),
            jnp.take(targets, slot_picks, axis=0),
            jnp.take(label_rows, slot_picks, axis=0),
            jnp.take(weights, slot_picks, axis=0),
            picked_now,
            pool_rows,
            pool_ids,
            factor,
        )
        grad_acc = grad_acc.at[picked_now.reshape(-1)].add(
            pool_grad.reshape((-1,) + pool_grad.shape[2:])
        )
        state_acc = state_acc.at[slot_picks].set(state_grad)
        return (loss_acc + jnp.sum(part_loss), grad_acc, state_acc)

    initial = (
        jnp.zeros((), jnp.float32),
        jnp.zeros(pool_rows.shape, jnp.float32),
        jnp.zeros(states.shape, jnp.float32),
    )
    return lax.fori_loop(0, rounds, advance, initial)


def per_device(hidden, target, pool_table, pool_items, labels, chosen, offsets):
    user_count = lax.axis_size("users")
    length = hidden.shape[1]
    features = hidden.shape[2]
    block_count = length // PB
    shard_rows, shard_items = (
        lax.all_gather(pool_table, "users", axis=0, tiled=True),
        lax.all_gather(pool_items, "users", axis=0, tiled=True),
    )
    pool_rows = shard_rows.reshape(-1, NB, features)
    pool_ids = shard_items.reshape(-1, NB)
    factor = 1.0 / (user_count * (offsets.shape[1] - 1))
    seq_place = lax.axis_index("seq")
    live_blocks = (offsets[0, -1] + PB - 1) // PB
    states = hidden.reshape(block_count, PB, features)
    targets = target.reshape(block_count, PB, features)
    label_rows = labels.reshape(block_count, PB)
    picked = chosen.reshape(block_count, chosen.shape[2])
    within = jnp.arange(PB, dtype=jnp.int32)
    slot_index = jnp.arange(block_count, dtype=jnp.int32)
    positions = seq_place * length + slot_index[:, None] * PB + within[None, :]
    weights = history_weights(offsets[0], positions)
    live_count = jnp.clip(live_blocks - seq_place * block_count, 0, block_count)
    loss_part, grad_pool, state_grad = run_blocks(
        states,
        targets,
        label_rows,
        weights,
        picked,
        slot_index,
        live_count,
        pool_rows,
        pool_ids,
        factor,
    )
    grad_hidden = state_grad.reshape(hidden.shape)
    loss_total = lax.psum(loss_part, ("seq", "users")) * factor
    grad_full = grad_pool.reshape(-1, features)
    owned_rows = lax.psum_scatter(grad_full, "users", scatter_dimension=0, tiled=True)
    grad_table = lax.psum(owned_rows, "seq")
    return (loss_total, grad_hidden, grad_table)


def solution(mesh):
    return jax.shard_map(
        per_device,
        mesh=mesh,
        in_specs=(
            P("users", "seq", None),
            P("users", "seq", None),
            P("users", None),
            P("users"),
            P("users", "seq"),
            P("users", "seq", None),
            P("users", None),
        ),
        out_specs=(P(), P("users", "seq", None), P("users", None)),
        check_vma=False,
    )
```

profile of v0, /device:TPU:1, one launch (start us, length us, event | category | flops | bytes accessed | tf_op | source)
XLA Modules:
  0.0 615.0 jit_solution(12936901382694185869)
XLA Ops:
  7.9 1.2 slice.11
  9.9 38.2 %all-gather = s32[32,1,256]{2,1,0:T(1,128)S(1)} all-gather(s32[1,1,256]{2,1,0:T(1,128)} %bitcast.72), channel_id=1, replica_groups=mesh['seq'=8,'users'=32] {'users'}, dimensions={0}, use_global_device_ids=true | all-gather | bytes 33792 | tf_op jit(solution)/shard_map/all_gather | solution.py:93
  48.1 1.7 convert.11
  49.9 0.8 convert_divide_fusion
  50.7 0.8 slice_bitcast_fusion.1
  51.7 59.8 %all-gather.3.cloned.1.call-done = bf16[8192,512]{1,0:T(8,128)(2,1)} async-done(((bf16[256,512]{1,0:T(8,128)(2,1)}), bf16[8192,512]{1,0:T(8,128)(2,1)}) %all-gather.3.cloned.1.call-update) | async-done | bytes 8388624 | tf_op jit(solution)/shard_map/all_gather | solution.py:92
  111.5 1.6 broadcast_in_dim.127
  113.1 7.9 %broadcast_in_dim.126 = f32[32,256,512]{2,1,0:T(8,128)} broadcast(f32[]{:T(128)} %copy.36), dimensions={} | broadcast | bytes 16777220 | tf_op jit(solution)/shard_map/broadcast_in_dim | solution.py:80
  120.9 164.0 %while.16 = (s32[]{:T(128)}, f32[]{:T(128)}, f32[32,256,512]{2,1,0:T(8,128)}, f32[8,128,512]{2,1,0:T(8,128)}, s32[]{:T(128)}, /*index=5*/s32[8]{0:T(128)S(1)}, f...) while((s32[]{:T(128)}, f32[]{:T(128)}, ...), condition=%wide.region_8.9_spmd, body=%wide.region_1.8_spmd.sunk | while | flops 3252174336 | bytes 194429456 | solution.py:83
  123.9 1.8 gather_fusion
  126.6 8.4 %gather_fusion.5 = bf16[32,256,512]{2,1,0:T(8,128)(2,1)} fusion(bf16[32,256,512]{2,1,0:T(8,128)(2,1)} %get-tuple-element.362, s32[1024]{0:T(1024)S(1)} %pad_clamp_fusion.5), kind=kCustom, calls=%fused_computation.6.clone.1 | custom fusion | bytes 16777344 | tf_op jit(solution)/shard_map/while/body/vmap(jit(_take))/gather | solution.py:20
  135.0 4.7 bitcast_select_fusion.3
  139.7 2.8 fusion.24
  142.9 1.9 copy-done
  144.8 1.0 fusion.25
  147.0 6.5 %convolution_add_fusion.2 = f32[4,128,512]{2,1,0:T(8,128)S(1)} fusion(bf16[4,2048,512]{2,1,0:T(8,128)(2,1)} %copy-done.1, f32[4,128]{1,0:T(4,128)S(1)} %get-tuple-element.315, bf16[4,128,512]{2,1,0:T(8,128)(2,1)S(1)} %gather_fusion, pred[4]{0:T(512)(128)(4,1)S(1)} %get-tuple-element.305, f32[4,128,2048]{2,1,0:T(8,128)} %copy-done, ...), kind=kOutput, calls=%fused_computation.17.clone.1 | convolution fusion | flops 1081081856 | bytes 14198788 | tf_op jit(solution)/shard_map/while/body/vmap()/dot_general | solution.py:35
  153.5 2.8 scatter_fusion.1
  156.3 10.4 %fusion.27 = f32[4,2048,512]{2,1,0:T(8,128)} fusion(bf16[4,128,512]{2,1,0:T(8,128)(2,1)S(1)} %get-tuple-element.308, f32[4,128,2048]{2,1,0:T(8,128)} %copy-done, f32[4,128]{1,0:T(4,128)S(1)} %get-tuple-element.313, f32[4,128]{1,0:T(4,128)S(1)} %get-tuple-element.314, f32[4,128]{1,0:T(4,128)S(1)} %max.31, s32[4,128]{1,0:T(4,128)S(1)} %broadcast_select_fusion.7, ...), kind=kOutput, calls=%fused_computation.40.clone.1 | convolution fusion | flops 1080033280 | bytes 21536768 | tf_op jit(solution)/shard_map/while/body/vmap()/dot_general | solution.py:38
  166.7 36.3 %scatter_fusion = f32[32,256,512]{2,1,0:T(8,128)} fusion(f32[32,256,512]{2,1,0:T(8,128)} %get-tuple-element.335, s32[32]{0:T(128)S(1)} %fusion.26, f32[32,256,512]{2,1,0:T(8,128)} %bitcast.60), kind=kCustom, calls=%fused_computation.7.clone.1 | custom fusion | flops 4194304 | bytes 50331776 | tf_op jit(solution)/shard_map/while/body/scatter-add | solution.py:72
  205.9 1.8 gather_fusion
  208.6 8.4 %gather_fusion.5 = bf16[32,256,512]{2,1,0:T(8,128)(2,1)} fusion(bf16[32,256,512]{2,1,0:T(8,128)(2,1)} %get-tuple-element.362, s32[1024]{0:T(1024)S(1)} %pad_clamp_fusion.5), kind=kCustom, calls=%fused_computation.6.clone.1 | custom fusion | bytes 16777344 | tf_op jit(solution)/shard_map/while/body/vmap(jit(_take))/gather | solution.py:20
  217.0 4.7 bitcast_select_fusion.3
  221.7 2.9 fusion.24
  224.9 1.9 copy-done
  226.8 1.0 fusion.25
  229.0 6.5 %convolution_add_fusion.2 = f32[4,128,512]{2,1,0:T(8,128)S(1)} fusion(bf16[4,2048,512]{2,1,0:T(8,128)(2,1)} %copy-done.1, f32[4,128]{1,0:T(4,128)S(1)} %get-tuple-element.315, bf16[4,128,512]{2,1,0:T(8,128)(2,1)S(1)} %gather_fusion, pred[4]{0:T(512)(128)(4,1)S(1)} %get-tuple-element.305, f32[4,128,2048]{2,1,0:T(8,128)} %copy-done, ...), kind=kOutput, calls=%fused_computation.17.clone.1 | convolution fusion | flops 1081081856 | bytes 14198788 | tf_op jit(solution)/shard_map/while/body/vmap()/dot_general | solution.py:35
  235.5 2.8 scatter_fusion.1
  238.2 10.4 %fusion.27 = f32[4,2048,512]{2,1,0:T(8,128)} fusion(bf16[4,128,512]{2,1,0:T(8,128)(2,1)S(1)} %get-tuple-element.308, f32[4,128,2048]{2,1,0:T(8,128)} %copy-done, f32[4,128]{1,0:T(4,128)S(1)} %get-tuple-element.313, f32[4,128]{1,0:T(4,128)S(1)} %get-tuple-element.314, f32[4,128]{1,0:T(4,128)S(1)} %max.31, s32[4,128]{1,0:T(4,128)S(1)} %broadcast_select_fusion.7, ...), kind=kOutput, calls=%fused_computation.40.clone.1 | convolution fusion | flops 1080033280 | bytes 21536768 | tf_op jit(solution)/shard_map/while/body/vmap()/dot_general | solution.py:38
  248.7 36.2 %scatter_fusion = f32[32,256,512]{2,1,0:T(8,128)} fusion(f32[32,256,512]{2,1,0:T(8,128)} %get-tuple-element.335, s32[32]{0:T(128)S(1)} %fusion.26, f32[32,256,512]{2,1,0:T(8,128)} %bitcast.60), kind=kCustom, calls=%fused_computation.7.clone.1 | custom fusion | flops 4194304 | bytes 50331776 | tf_op jit(solution)/shard_map/while/body/scatter-add | solution.py:72
  285.0 240.3 %reduce-scatter.2.cloned.1.call-done = f32[256,512]{1,0:T(8,128)} async-done(((f32[8192,512]{1,0:T(8,128)}), f32[256,512]{1,0:T(8,128)}) %reduce-scatter.2.cloned.1.call-update) | async-done | bytes 524304 | tf_op jit(solution)/shard_map/reduce_scatter | solution.py:124
  525.3 79.5 %psum.14 = f32[]{:T(128)} all-reduce(f32[]{:T(128)} %get-tuple-element.169), channel_id=1, replica_groups=mesh['seq'=8,'users'=32] {'seq','users'}, use_global_device_ids=true, to_apply=%region_9.10 | all-reduce | flops 1 | bytes 8 | tf_op jit(solution)/shard_map/psum | solution.py:122
  605.5 1.9 copy.37
  (64 shorter events, 10.7 us)
Async XLA Ops:
  7.2 104.3 %all-gather.3.cloned.1.call-start = ((), (), s32[]{:S(2)}) async-start(), calls=%async_computation.1 | async-start | bytes 8650752 | tf_op jit(solution)/shard_map/all_gather | solution.py:92
  7.9 517.4 %reduce-scatter.2.cloned.1.call-start = ((), (), s32[]{:S(2)}) async-start(), calls=%async_computation.2 | async-start | bytes 17301504 | tf_op jit(solution)/shard_map/reduce_scatter | solution.py:124
  113.1 7.9 %copy-start.2 = (s32[1,8,8]{2,1,0:T(8,128)S(1)}, s32[1,8,8]{2,1,0:T(8,128)}, u32[]{:S(2)}) copy-start(s32[1,8,8]{2,1,0:T(8,128)} %param.14) | copy-start | bytes 772
  113.1 7.9 %copy-start.3 = (s32[1,1024]{1,0:T(1,128)S(1)}, s32[1,1024]{1,0:T(1,128)}, u32[]{:S(2)}) copy-start(s32[1,1024]{1,0:T(1,128)} %param.13) | copy-start | bytes 12292
  139.7 3.2 copy-start.1
  142.9 1.9 copy-start
  221.7 3.2 copy-start.1
  224.9 1.9 copy-start
  284.9 320.6 %all-reduce.2.cloned.1.call-start = ((), (), s32[]{:S(2)}) async-start(), calls=%async_computation.3 | async-start | bytes 1048576 | tf_op jit(solution)/shard_map/psum | solution.py:125
Sparse Core Ops, SparseCore 0:
  10.6 100.8 all-gather.2
  285.0 240.2 reduce-scatter.1
  527.6 66.9 all-reduce.1
where the time goes:
time: 616 us; the launch traced here: 615 us
  waiting for transfers between devices  301 us (49%)
  blocking collectives  118 us (19%)
  other arithmetic  89.2 us (14%)
  local copies, waits for them, and re-layouts  50.1 us (8%)
  matrix products  39.5 us (6%)
  between operations  16.2 us (3%)
    reduce_scatter x1, waiting for transfers between devices, per_device(): lax.psum_scatter(grad_full, 'users', scatter_dimension=0, tiled=True)  240 us
    psum x1, blocking collectives, per_device(): loss_total = lax.psum(loss_part, ('seq', 'users')) * factor  79.5 us
    scatter-add x2, other arithmetic, advance(): grad_acc.at[picked_now.reshape(-1)]  72.5 us
    all_gather x1, waiting for transfers between devices, per_device(): lax.all_gather(pool_table, 'users', axis=0, tiled=True)  59.8 us
    all_gather x1, blocking collectives, per_device(): lax.all_gather(pool_items, 'users', axis=0, tiled=True)  38.2 us
    dot_general x2, matrix products, block_terms(): pool_grad = jnp.dot(neg_grad.T, narrow, preferred_element_type=jnp.float32)  20.9 us
    gather x2, local copies, waits for them, and re-layouts, block_terms(): jnp.take(pool_rows, chosen, axis=0).reshape(-1, pool_rows.shape[2])  16.8 us
    dot_general x2, matrix products, block_terms(): jnp.dot(neg_grad, negatives, preferred_element_type=jnp.float32)  12.9 us
  transfers between devices with their start and end apart: 3, of which 2 were waited for; matrix products, arithmetic and copies ran while one was open for 1% of the time, Pallas kernels for 0%

commit v1 on v0

--- a/solution.py
+++ b/solution.py
@@ -1,3 +1,4 @@
+import functools
 import jax
 import jax.numpy as jnp
 from jax import lax
@@ -5,6 +6,17 @@
 
 NB = 256
 PB = 128
+
+
+def _show_notes(tile_in, bus_axis):
+    before = lax.axis_size(bus_axis)
+    tall = jnp.stack([tile_in] * before)
+    value_now = lax.all_to_all(tall, bus_axis, 0, 0)
+    carry_out = jnp.concatenate(value_now, 0)
+    return carry_out
+
+
+update_tokens = functools.partial(_show_notes, bus_axis="users")
 
 
 def history_weights(bounds, positions):
@@ -90,7 +102,7 @@
     block_count = length // PB
     shard_rows, shard_items = (
         lax.all_gather(pool_table, "users", axis=0, tiled=True),
-        lax.all_gather(pool_items, "users", axis=0, tiled=True),
+        update_tokens(pool_items),
     )
     pool_rows = shard_rows.reshape(-1, NB, features)
     pool_ids = shard_items.reshape(-1, NB)

time: 616 us -> 617 us (level)
  blocking collectives: 118 us -> 79.7 us
  waiting for transfers between devices: 301 us -> 327 us
  starting transfers between devices: 0.12 us -> 12 us
    all_gather x1 -> x0, blocking collectives: 38.2 us -> none  [per_device(): lax.all_gather(pool_items, 'users', axis=0, tiled=True)]
    all_gather x1, waiting for transfers between devices: 59.8 us -> 81.6 us  [per_device(): lax.all_gather(pool_table, 'users', axis=0, tiled=True)]
    all_to_all x0 -> x1, starting transfers between devices: none -> 11.9 us  [_show_notes(): value_now = lax.all_to_all(tall, bus_axis, 0, 0)]
  transfers between devices with their start and end apart: 3 -> 4, of which waited for: 2 -> 3; matrix products, arithmetic and copies ran while one was open for 1% -> 1% of each run, Pallas kernels for 0% -> 0%
where the time goes in v1:
time: 617 us; the launch traced here: 616 us
  waiting for transfers between devices  327 us (53%)
  other arithmetic  89.2 us (14%)
  blocking collectives  79.7 us (13%)
  local copies, waits for them, and re-layouts  51.4 us (8%)
  matrix products  39.5 us (6%)
  between operations  16.3 us (3%)
  starting transfers between devices  12 us (2%)
    reduce_scatter x1, waiting for transfers between devices, per_device(): lax.psum_scatter(grad_full, 'users', scatter_dimension=0, tiled=True)  241 us
    all_gather x1, waiting for transfers between devices, per_device(): lax.all_gather(pool_table, 'users', axis=0, tiled=True)  81.6 us
    psum x1, blocking collectives, per_device(): loss_total = lax.psum(loss_part, ('seq', 'users')) * factor  79.7 us
    scatter-add x2, other arithmetic, advance(): grad_acc.at[picked_now.reshape(-1)]  72.5 us
    dot_general x2, matrix products, block_terms(): pool_grad = jnp.dot(neg_grad.T, narrow, preferred_element_type=jnp.float32)  20.9 us
    gather x2, local copies, waits for them, and re-layouts, block_terms(): jnp.take(pool_rows, chosen, axis=0).reshape(-1, pool_rows.shape[2])  16.8 us
    dot_general x2, matrix products, block_terms(): jnp.dot(neg_grad, negatives, preferred_element_type=jnp.float32)  12.9 us
  transfers between devices with their start and end apart: 4, of which 3 were waited for; matrix products, arithmetic and copies ran while one was open for 1% of the time, Pallas kernels for 0%

profile of v1, /device:TPU:1, one launch (start us, length us, event | category | flops | bytes accessed | tf_op | source)
XLA Modules:
  0.0 616.1 jit_solution(3176089327698085235)
XLA Ops:
  7.9 1.3 stack.2
  9.2 11.9 %all-to-all-start = ((s32[32,1,256]{2,1,0:T(1,128)}), s32[32,1,256]{2,1,0:T(1,128)S(1)}, u32[]{:S(2)}, u32[]{:S(2)}) async-start(s32[32,1,256]{2,1,0:T(1,128)} %stack.2), calls=%async_computation | async-start | bytes 65536 | tf_op jit(solution)/shard_map/all_to_all | solution.py:14
  21.1 1.2 slice.11
  23.0 1.7 convert.11
  26.6 3.3 all-to-all-done
  29.8 81.6 %all-gather.2.cloned.1.call-done = bf16[8192,512]{1,0:T(8,128)(2,1)} async-done(((bf16[256,512]{1,0:T(8,128)(2,1)}), bf16[8192,512]{1,0:T(8,128)(2,1)}) %all-gather.2.cloned.1.call-update) | async-done | bytes 8388624 | tf_op jit(solution)/shard_map/all_gather | solution.py:104
  111.5 1.6 broadcast_in_dim.127
  113.0 7.9 %broadcast_in_dim.126 = f32[32,256,512]{2,1,0:T(8,128)} broadcast(f32[]{:T(128)} %copy.36), dimensions={} | broadcast | bytes 16777220 | tf_op jit(solution)/shard_map/broadcast_in_dim | solution.py:92
  120.9 164.2 %while.16 = (s32[]{:T(128)}, f32[]{:T(128)}, f32[32,256,512]{2,1,0:T(8,128)}, f32[8,128,512]{2,1,0:T(8,128)}, s32[]{:T(128)}, /*index=5*/s32[8]{0:T(128)S(1)}, f...) while((s32[]{:T(128)}, f32[]{:T(128)}, ...), condition=%wide.region_8.9_spmd, body=%wide.region_1.8_spmd.sunk | while | flops 3252174336 | bytes 194429456 | solution.py:95
  123.8 1.8 gather_fusion
  126.6 8.4 %gather_fusion.5 = bf16[32,256,512]{2,1,0:T(8,128)(2,1)} fusion(bf16[32,256,512]{2,1,0:T(8,128)(2,1)} %get-tuple-element.362, s32[1024]{0:T(1024)S(1)} %pad_clamp_fusion.5), kind=kCustom, calls=%fused_computation.6.clone.1 | custom fusion | bytes 16777344 | tf_op jit(solution)/shard_map/while/body/vmap(jit(_take))/gather | solution.py:32
  135.0 4.7 bitcast_select_fusion.3
  139.7 2.8 fusion.24
  142.9 1.9 copy-done
  144.8 1.0 fusion.25
  147.1 6.5 %convolution_add_fusion.2 = f32[4,128,512]{2,1,0:T(8,128)S(1)} fusion(bf16[4,2048,512]{2,1,0:T(8,128)(2,1)} %copy-done.1, f32[4,128]{1,0:T(4,128)S(1)} %get-tuple-element.315, bf16[4,128,512]{2,1,0:T(8,128)(2,1)S(1)} %gather_fusion, pred[4]{0:T(512)(128)(4,1)S(1)} %get-tuple-element.305, f32[4,128,2048]{2,1,0:T(8,128)} %copy-done, ...), kind=kOutput, calls=%fused_computation.17.clone.1 | convolution fusion | flops 1081081856 | bytes 14198788 | tf_op jit(solution)/shard_map/while/body/vmap()/dot_general | solution.py:47
  153.6 2.8 scatter_fusion.1
  156.3 10.4 %fusion.27 = f32[4,2048,512]{2,1,0:T(8,128)} fusion(bf16[4,128,512]{2,1,0:T(8,128)(2,1)S(1)} %get-tuple-element.308, f32[4,128,2048]{2,1,0:T(8,128)} %copy-done, f32[4,128]{1,0:T(4,128)S(1)} %get-tuple-element.313, f32[4,128]{1,0:T(4,128)S(1)} %get-tuple-element.314, f32[4,128]{1,0:T(4,128)S(1)} %max.31, s32[4,128]{1,0:T(4,128)S(1)} %broadcast_select_fusion.7, ...), kind=kOutput, calls=%fused_computation.40.clone.1 | convolution fusion | flops 1080033280 | bytes 21536768 | tf_op jit(solution)/shard_map/while/body/vmap()/dot_general | solution.py:50
  166.8 36.3 %scatter_fusion = f32[32,256,512]{2,1,0:T(8,128)} fusion(f32[32,256,512]{2,1,0:T(8,128)} %get-tuple-element.335, s32[32]{0:T(128)S(1)} %fusion.26, f32[32,256,512]{2,1,0:T(8,128)} %bitcast.59), kind=kCustom, calls=%fused_computation.7.clone.1 | custom fusion | flops 4194304 | bytes 50331776 | tf_op jit(solution)/shard_map/while/body/scatter-add | solution.py:84
  206.0 1.8 gather_fusion
  208.7 8.4 %gather_fusion.5 = bf16[32,256,512]{2,1,0:T(8,128)(2,1)} fusion(bf16[32,256,512]{2,1,0:T(8,128)(2,1)} %get-tuple-element.362, s32[1024]{0:T(1024)S(1)} %pad_clamp_fusion.5), kind=kCustom, calls=%fused_computation.6.clone.1 | custom fusion | bytes 16777344 | tf_op jit(solution)/shard_map/while/body/vmap(jit(_take))/gather | solution.py:32
  217.1 4.7 bitcast_select_fusion.3
  221.8 2.8 fusion.24
  225.0 1.9 copy-done
  226.9 1.0 fusion.25
  229.2 6.5 %convolution_add_fusion.2 = f32[4,128,512]{2,1,0:T(8,128)S(1)} fusion(bf16[4,2048,512]{2,1,0:T(8,128)(2,1)} %copy-done.1, f32[4,128]{1,0:T(4,128)S(1)} %get-tuple-element.315, bf16[4,128,512]{2,1,0:T(8,128)(2,1)S(1)} %gather_fusion, pred[4]{0:T(512)(128)(4,1)S(1)} %get-tuple-element.305, f32[4,128,2048]{2,1,0:T(8,128)} %copy-done, ...), kind=kOutput, calls=%fused_computation.17.clone.1 | convolution fusion | flops 1081081856 | bytes 14198788 | tf_op jit(solution)/shard_map/while/body/vmap()/dot_general | solution.py:47
  235.7 2.8 scatter_fusion.1
  238.4 10.4 %fusion.27 = f32[4,2048,512]{2,1,0:T(8,128)} fusion(bf16[4,128,512]{2,1,0:T(8,128)(2,1)S(1)} %get-tuple-element.308, f32[4,128,2048]{2,1,0:T(8,128)} %copy-done, f32[4,128]{1,0:T(4,128)S(1)} %get-tuple-element.313, f32[4,128]{1,0:T(4,128)S(1)} %get-tuple-element.314, f32[4,128]{1,0:T(4,128)S(1)} %max.31, s32[4,128]{1,0:T(4,128)S(1)} %broadcast_select_fusion.7, ...), kind=kOutput, calls=%fused_computation.40.clone.1 | convolution fusion | flops 1080033280 | bytes 21536768 | tf_op jit(solution)/shard_map/while/body/vmap()/dot_general | solution.py:50
  248.9 36.2 %scatter_fusion = f32[32,256,512]{2,1,0:T(8,128)} fusion(f32[32,256,512]{2,1,0:T(8,128)} %get-tuple-element.335, s32[32]{0:T(128)S(1)} %fusion.26, f32[32,256,512]{2,1,0:T(8,128)} %bitcast.59), kind=kCustom, calls=%fused_computation.7.clone.1 | custom fusion | flops 4194304 | bytes 50331776 | tf_op jit(solution)/shard_map/while/body/scatter-add | solution.py:84
  285.2 241.0 %reduce-scatter.2.cloned.1.call-done = f32[256,512]{1,0:T(8,128)} async-done(((f32[8192,512]{1,0:T(8,128)}), f32[256,512]{1,0:T(8,128)}) %reduce-scatter.2.cloned.1.call-update) | async-done | bytes 524304 | tf_op jit(solution)/shard_map/reduce_scatter | solution.py:136
  526.2 79.7 %psum.14 = f32[]{:T(128)} all-reduce(f32[]{:T(128)} %get-tuple-element.169), channel_id=1, replica_groups=mesh['seq'=8,'users'=32] {'seq','users'}, use_global_device_ids=true, to_apply=%region_9.10 | all-reduce | flops 1 | bytes 8 | tf_op jit(solution)/shard_map/psum | solution.py:134
  606.6 1.9 copy.37
  (66 shorter events, 12.4 us)
Async XLA Ops:
  7.2 104.3 %all-gather.2.cloned.1.call-start = ((), (), s32[]{:S(2)}) async-start(), calls=%async_computation.2 | async-start | bytes 8650752 | tf_op jit(solution)/shard_map/all_gather | solution.py:104
  9.2 20.6 %all-to-all-start = ((s32[32,1,256]{2,1,0:T(1,128)}), s32[32,1,256]{2,1,0:T(1,128)S(1)}, u32[]{:S(2)}, u32[]{:S(2)}) async-start(s32[32,1,256]{2,1,0:T(1,128)} %stack.2), calls=%async_computation | async-start | bytes 65536 | tf_op jit(solution)/shard_map/all_to_all | solution.py:14
  21.1 505.1 %reduce-scatter.2.cloned.1.call-start = ((), (), s32[]{:S(2)}) async-start(), calls=%async_computation.3 | async-start | bytes 17301504 | tf_op jit(solution)/shard_map/reduce_scatter | solution.py:136
  113.0 7.9 %copy-start.2 = (s32[1,8,8]{2,1,0:T(8,128)S(1)}, s32[1,8,8]{2,1,0:T(8,128)}, u32[]{:S(2)}) copy-start(s32[1,8,8]{2,1,0:T(8,128)} %param.14) | copy-start | bytes 772
  113.0 7.9 %copy-start.3 = (s32[1,1024]{1,0:T(1,128)S(1)}, s32[1,1024]{1,0:T(1,128)}, u32[]{:S(2)}) copy-start(s32[1,1024]{1,0:T(1,128)} %param.13) | copy-start | bytes 12292
  139.7 3.2 copy-start.1
  142.9 1.9 copy-start
  221.8 3.2 copy-start.1
  225.0 1.9 copy-start
  285.1 321.4 %all-reduce.2.cloned.1.call-start = ((), (), s32[]{:S(2)}) async-start(), calls=%async_computation.4 | async-start | bytes 1048576 | tf_op jit(solution)/shard_map/psum | solution.py:137
Sparse Core Ops, SparseCore 0:
  10.6 100.8 all-gather.1
  285.2 240.8 reduce-scatter.1
  528.5 66.9 all-reduce.1
